TPU v7x, 32 devices: a whole 2x2x4 slice. The times are simulated.
32 devices in a mesh: dp: 4 (over x, core), expert: 8 (over z, y).
Axes of the slice: x: 2, y: 2, z: 4, core: 2. Of those that a mesh axis runs over, the one named last changes fastest.
Arguments:
- hidden: bfloat16 [2048, 8, 1536], P(('dp', 'expert')), may hold values from -6 to 6
- routes: int32 [2048, 8], P(('dp', 'expert')), may hold values from 0 to 15, all different within a row; in each aligned block of 64 rows (0 to 63, 64 to 127, ...) at most 48 rows name the same one
- gate_scores: int32 [2048, 8], P(('dp', 'expert')), may hold values from 1 to 64
- down_weight: bfloat16 [16, 1536, 4096], P('expert', None, 'dp'), may hold values from -0.15625 to 0.15625
Outputs:
- output: bfloat16 [2048, 4096], P(('dp', 'expert'))
- gram: float32 [16, 1536, 1536], P('expert', 'dp')
Inputs may be any that keep to these rules, and one draw needn't show every extreme that they name: `routes`: each token names 8 different experts. Among the 64 tokens of one device no expert is named more than 48 times, and on some devices one expert is named exactly 48 times. Every expert is named by some token.
All inputs are finite; a program needn't handle non-finite values.
Results may differ from a plain program's by a relative error of at most 0.005.
Values may be sent and summed in bfloat16 or wider, within the bound.
A program may use at most 128 MiB of HBM per device.

v0:
```python
import jax
import jax.numpy as jnp
from jax import lax
from jax.sharding import PartitionSpec as P


def local(hidden, routes, gate_scores, down_weight):
    tokens = hidden.shape[0]
    top_count = hidden.shape[1]
    hidden_width = hidden.shape[2]
    n_owner = lax.axis_size("expert")
    n_group = lax.axis_size("dp")
    per_owner = down_weight.shape[0]
    experts = n_owner * per_owner
    pair_total = tokens * top_count
    capacity = 3 * tokens * top_count // (2 * experts)
    flat_routes = routes.reshape(pair_total)
    onehot = (flat_routes[:, None] == jnp.arange(experts, dtype=jnp.int32)[None, :]).astype(
        jnp.int32
    )
    before = jnp.cumsum(onehot, axis=0) - onehot
    position = jnp.sum(before * onehot, axis=1)
    slot_index = flat_routes * capacity + position
    local_counts = jnp.sum(onehot, axis=0).astype(jnp.float32)
    totals = lax.psum(local_counts, ("dp", "expert"))
    pair_rows = hidden.reshape(pair_total, hidden_width)
    outgoing = (
        jnp.zeros((experts * capacity, hidden_width), jnp.bfloat16).at[slot_index].set(pair_rows)
    )
    outgoing = outgoing.reshape(n_owner, per_owner, capacity, hidden_width)
    arrived = lax.all_to_all(outgoing, "expert", split_axis=0, concat_axis=0, tiled=True)
    everyone = lax.all_gather(arrived, "dp", axis=0, tiled=True)
    own_counts = lax.dynamic_slice_in_dim(
        totals, lax.axis_index("expert") * per_owner, per_owner, 0
    )
    block_width = hidden_width // n_group
    my_columns = lax.dynamic_slice_in_dim(
        everyone, lax.axis_index("dp") * block_width, block_width, 3
    )
    gram_rows = jnp.einsum(
        "sxcf,sxcg->xfg", my_columns, everyone, preferred_element_type=jnp.float32
    )
    results = jnp.einsum(
        "sxcf,xfd->sxcd", everyone, down_weight, preferred_element_type=jnp.float32
    ).astype(jnp.bfloat16)
    returned = lax.all_to_all(
        lax.all_to_all(results, "dp", split_axis=0, concat_axis=3, tiled=True),
        "expert",
        split_axis=0,
        concat_axis=0,
        tiled=True,
    )
    gram = gram_rows / own_counts[:, None, None]
    model_width = returned.shape[3]
    pair_results = returned.reshape(experts * capacity, model_width)[slot_index]
    scores = gate_scores.astype(jnp.float32)
    weight = scores / jnp.sum(scores, axis=1, keepdims=True)
    combined = jnp.sum(
        pair_results.reshape(tokens, top_count, model_width).astype(jnp.float32)
        * weight[:, :, None],
        axis=1,
    )
    return (combined.astype(jnp.bfloat16), gram)


def solution(mesh):
    placed = (
        P(("dp", "expert"), None, None),
        P(("dp", "expert"), None),
        P(("dp", "expert"), None),
        P("expert", None, "dp"),
    )
    return jax.shard_map(
        local,
        mesh=mesh,
        in_specs=placed,
        out_specs=(P(("dp", "expert"), None), P("expert", "dp", None)),
        check_vma=False,
    )
```

profile of v0, /device:TPU:0, one launch (start us, length us, event | category | flops | bytes accessed | tf_op | source)
XLA Modules:
  0.0 453.1 jit_solution(3097682405529023763)
XLA Ops:
  7.2 0.9 copy.15
  8.1 0.1 eq.29
  8.2 0.1 eq.25
  8.3 0.7 broadcast_multiply_fusion
  9.0 1.1 reduce-window.6
  10.1 0.2 slice_reduce_fusion
  10.4 0.1 copy.14
  10.5 0.1 mul.35
  10.6 0.1 convert_reduce_fusion
  10.7 4.7 %scatter_custom_fusion = bf16[768,1536]{1,0:T(8,128)(2,1)} fusion(s32[512]{0:T(512)S(1)} %bitcast.42, bf16[64,8,1536]{2,1,0:T(8,128)(2,1)S(1)} %copy-done, bf16[]{:T(256)} %constant.11.clone.1), kind=kCustom, calls=%fused_computation.10 | custom fusion | bytes 3932162 | tf_op jit(solution)/shard_map/scatter | solution.py:28
  15.4 61.2 %all_to_all.28 = bf16[8,2,48,1536]{3,2,1,0:T(8,128)(2,1)S(1)} all-to-all(bf16[8,2,48,1536]{3,2,1,0:T(8,128)(2,1)} %bitcast.41), channel_id=1, replica_groups=mesh['dp'=4,'expert'=8] {'expert'}, dimensions={0} | all-to-all | bytes 4718592 | tf_op jit(solution)/shard_map/all_to_all | solution.py:31
  76.6 1.6 copy.18
  78.2 63.4 %all-gather.2.cloned.1.call-done = bf16[32,2,48,1536]{3,2,0,1:T(8,128)(2,1)} async-done(((bf16[8,2,48,1536]{3,2,0,1:T(8,128)(2,1)}), bf16[32,2,48,1536]{3,2,0,1:T(8,128)(2,1)}) %all-gather.2.cloned.1.call-update) | async-done | bytes 9437200 | tf_op jit(solution)/shard_map/all_gather | solution.py:32
  141.5 14.3 %convert_bitcast_fusion = bf16[32,2,48,1024]{3,2,0,1:T(8,128)(2,1)S(1)} fusion(bf16[32,2,48,1536]{3,2,0,1:T(8,128)(2,1)} %all-gather.2.cloned.1.call-done, bf16[2,1536,1024]{2,1,0:T(8,128)(2,1)} %param.7), kind=kOutput, calls=%fused_computation.7 | convolution fusion | flops 9666822144 | bytes 22020096 | tf_op jit(solution)/shard_map/sxcf,xfd->sxcd/dot_general | solution.py:43
  155.9 1.3 copy.19
  157.2 74.2 %all_to_all.29 = bf16[32,2,48,1024]{3,2,1,0:T(8,128)(2,1)} all-to-all(bf16[32,2,48,1024]{3,2,1,0:T(8,128)(2,1)S(1)} %copy.19), channel_id=1, replica_groups=mesh['dp'=4,'expert'=8] {'dp'}, dimensions={0} | all-to-all | bytes 12582912 | tf_op jit(solution)/shard_map/all_to_all | solution.py:47
  231.4 10.8 %copy.27 = bf16[4,8,2,48,1024]{4,0,3,2,1:T(4,128)(2,1)} copy(bf16[4,8,2,48,1024]{4,3,2,1,0:T(8,128)(2,1)} %bitcast.39) | data formatting | bytes 12582912 | tf_op jit(solution)/shard_map/all_to_all | solution.py:47
  242.2 11.1 %all_to_all.23 = bf16[8,2,48,4096]{3,2,1,0:T(8,128)(2,1)} reshape(bf16[8,2,48,4,1024]{4,3,2,1,0:T(4,128)(2,1)} %bitcast.40) | data formatting | bytes 12582912 | tf_op jit(solution)/shard_map/all_to_all | solution.py:47
  253.2 5.6 %all-to-all-start.2 = ((bf16[8,2,48,4096]{3,2,1,0:T(8,128)(2,1)}), bf16[8,2,48,4096]{3,2,1,0:T(8,128)(2,1)}, u32[]{:S(2)}, u32[]{:S(2)}) async-start(bf16[8,2,48,4096]{3,2,1,0:T(8,128)(2,1)} %all_to_all.23), calls=%async_computation.2 | async-start | bytes 12582912 | tf_op jit(solution)/shard_map/all_to_all | solution.py:46
  258.9 157.9 %psum.7 = f32[16]{0:T(128)S(1)} all-reduce(f32[16]{0:T(128)S(1)} %convert_element_type.36), channel_id=1, replica_groups=mesh['dp'=4,'expert'=8] {'dp','expert'}, use_global_device_ids=true, to_apply=%region_7.8 | all-reduce | flops 16 | bytes 128 | tf_op jit(solution)/shard_map/psum | solution.py:25
  416.8 0.1 copy.21
  417.0 10.5 %bitcast_divide_fusion = f32[2,384,1536]{2,1,0:T(8,128)} fusion(bf16[32,2,48,1536]{3,2,0,1:T(8,128)(2,1)} %all-gather.2.cloned.1.call-done, f32[2]{0:T(128)S(1)} %dynamic_slice.7, s32[]{:T(128)S(6)} %select_n.18), kind=kOutput, calls=%fused_computation.8 | convolution fusion | flops 3625058304 | bytes 16515084 | tf_op jit(solution)/shard_map/sxcf,sxcg->xfg/dot_general | solution.py:40
  427.5 12.3 %gather_fusion = bf16[512,4096]{1,0:T(8,128)(2,1)} fusion(bf16[768,4096]{1,0:T(8,128)(2,1)} %bitcast.10, s32[1024]{0:T(1024)S(1)} %pad_clamp_fusion), kind=kCustom, calls=%fused_computation | custom fusion | bytes 8390656 | tf_op jit(solution)/shard_map/gather | solution.py:55
  439.8 6.5 %fusion = bf16[64,4096]{1,0:T(8,128)(2,1)} fusion(bf16[512,4096]{1,0:T(8,128)(2,1)} %gather_fusion, f32[64,8]{1,0:T(8,128)S(1)} %copy.21), kind=kLoop, calls=%fused_computation.3 | loop fusion | flops 6029312 | bytes 4720640 | tf_op jit(solution)/shard_map/reduce_sum | solution.py:58
  (18 shorter events, 0.2 us)
Async XLA Ops:
  7.2 3.6 copy-start
  7.2 134.4 %all-gather.2.cloned.1.call-start = ((), (), s32[]{:S(2)}) async-start(), calls=%async_computation.3 | async-start | bytes 11796480 | tf_op jit(solution)/shard_map/all_gather | solution.py:32
  253.2 163.6 %copy-start.2 = (s32[64,8]{0,1:T(8,128)S(1)}, s32[64,8]{0,1:T(8,128)}, u32[]{:S(2)}) copy-start(s32[64,8]{0,1:T(8,128)} %param.6) | copy-start | bytes 6148
  253.2 174.3 %all-to-all-start.2 = ((bf16[8,2,48,4096]{3,2,1,0:T(8,128)(2,1)}), bf16[8,2,48,4096]{3,2,1,0:T(8,128)(2,1)}, u32[]{:S(2)}, u32[]{:S(2)}) async-start(bf16[8,2,48,4096]{3,2,1,0:T(8,128)(2,1)} %all_to_all.23), calls=%async_computation.2 | async-start | bytes 12582912 | tf_op jit(solution)/shard_map/all_to_all | solution.py:46
  427.5 18.7 %copy-start.1 = (bf16[64,8,1536]{2,1,0:T(8,128)(2,1)S(1)}, bf16[64,8,1536]{2,1,0:T(8,128)(2,1)}, u32[]{:S(2)}) copy-start(bf16[64,8,1536]{2,1,0:T(8,128)(2,1)} %param.4) | copy-start | bytes 4718596
Sparse Core Ops, SparseCore 0:
  78.3 63.2 all-gather.1
where the time goes:
time: 454 us; the launch traced here: 453 us
  blocking collectives  293 us (65%)
  waiting for transfers between devices  63.4 us (14%)
  local copies, waits for them, and re-layouts  43.3 us (10%)
  matrix products  24.8 us (5%)
  between operations  14.1 us (3%)
  other arithmetic  8.53 us (2%)
  starting transfers between devices  5.69 us (1%)
    psum x1, blocking collectives, local(): totals = lax.psum(local_counts, ('dp', 'expert'))  158 us
    all_to_all x1, blocking collectives, local(): lax.all_to_all(results, 'dp', split_axis=0, concat_axis=3, tiled=True)  74.2 us
    all_gather x1, waiting for transfers between devices, local(): everyone = lax.all_gather(arrived, 'dp', axis=0, tiled=True)  63.4 us
    all_to_all x1, blocking collectives, local(): lax.all_to_all(outgoing, 'expert', split_axis=0, concat_axis=0, tiled=True)  61.2 us
    all_to_all x2, local copies, waits for them, and re-layouts, local(): lax.all_to_all(results, 'dp', split_axis=0, concat_axis=3, tiled=True)  21.9 us
    dot_general x1, matrix products, local(): jnp.einsum('sxcf,xfd->sxcd', everyone, down_weight, preferred_element_typ...  14.3 us
    gather x1, local copies, waits for them, and re-layouts, local(): pair_results = returned.reshape(experts * capacity, model_width)[slot_index]  12.3 us
    dot_general x1, matrix products, local(): jnp.einsum('sxcf,sxcg->xfg', my_columns, everyone, preferred_element_type...  10.5 us
  transfers between devices with their start and end apart: 2, of which 1 were waited for; matrix products, arithmetic and copies ran while one was open for 2% of the time, Pallas kernels for 0%

commit v1 on v0

--- a/solution.py
+++ b/solution.py
@@ -2,6 +2,29 @@
 import jax.numpy as jnp
 from jax import lax
 from jax.sharding import PartitionSpec as P
+
+
+def in_blocks(x, dim, size):
+    lengths = x.shape
+    pieces = x.reshape(*lengths[:dim], size, lengths[dim] // size, *lengths[dim + 1 :])
+    return jnp.moveaxis(pieces, dim, 0)
+
+
+def laid_out(blocks, dim):
+    blocks = jnp.moveaxis(blocks, 0, dim)
+    dims = blocks.shape
+    return blocks.reshape(*dims[:dim], dims[dim] * dims[dim + 1], *dims[dim + 2 :])
+
+
+def exchange_directly(x, axis, split_dim, concat_dim):
+    peers, mine = (lax.axis_size(axis), lax.axis_index(axis))
+    blocks = in_blocks(x, split_dim, peers)
+    done = [blocks[mine]]
+    for lap in range(1, peers):
+        sent = blocks[(mine + lap) % peers]
+        done.append(lax.ppermute(sent, axis, [(i, (i + lap) % peers) for i in range(peers)]))
+    blocks = jnp.stack(done)[(mine - jnp.arange(peers)) % peers]
+    return laid_out(blocks, concat_dim)
 
 
 def local(hidden, routes, gate_scores, down_weight):
@@ -28,7 +51,7 @@
         jnp.zeros((experts * capacity, hidden_width), jnp.bfloat16).at[slot_index].set(pair_rows)
     )
     outgoing = outgoing.reshape(n_owner, per_owner, capacity, hidden_width)
-    arrived = lax.all_to_all(outgoing, "expert", split_axis=0, concat_axis=0, tiled=True)
+    arrived = exchange_directly(outgoing, "expert", 0, 0)
     everyone = lax.all_gather(arrived, "dp", axis=0, tiled=True)
     own_counts = lax.dynamic_slice_in_dim(
         totals, lax.axis_index("expert") * per_owner, per_owner, 0

time: 454 us -> 468 us (1.031)
  blocking collectives: 293 us -> 232 us
  waiting for transfers between devices: 63.4 us -> 109 us
  starting transfers between devices: 5.69 us -> 22.5 us
  local copies, waits for them, and re-layouts: 43.3 us -> 56.3 us
    all_to_all x1 -> x0, blocking collectives: 61.2 us -> none  [local(): lax.all_to_all(outgoing, 'expert', split_axis=0, concat_axis=0, tiled=True)]
    ppermute x0 -> x7, waiting for transfers between devices: none -> 38.7 us  [exchange_directly(): lax.ppermute(sent, axis, [(i, (i + lap) % peers) for i in range(peers)])]
    ppermute x0 -> x7, starting transfers between devices: none -> 16.8 us  [exchange_directly(): lax.ppermute(sent, axis, [(i, (i + lap) % peers) for i in range(peers)])]
    gather x0 -> x2, local copies, waits for them, and re-layouts: none -> 7 us  [exchange_directly(): blocks = jnp.stack(done)[(mine - jnp.arange(peers)) % peers]]
    all_gather x1, waiting for transfers between devices: 63.4 us -> 70.2 us  [local(): everyone = lax.all_gather(arrived, 'dp', axis=0, tiled=True)]
  transfers between devices with their start and end apart: 2 -> 9, of which waited for: 1 -> 5; matrix products, arithmetic and copies ran while one was open for 2% -> 3% of each run, Pallas kernels for 0% -> 0%
where the time goes in v1:
time: 468 us
  blocking collectives  232 us (50%)
  waiting for transfers between devices  109 us (23%)
  local copies, waits for them, and re-layouts  56.3 us (12%)
  matrix products  24.8 us (5%)
  starting transfers between devices  22.5 us (5%)
  between operations  14.2 us (3%)
  other arithmetic  8.64 us (2%)
    psum x1, blocking collectives, local(): totals = lax.psum(local_counts, ('dp', 'expert'))  158 us
    all_to_all x1, blocking collectives, local(): lax.all_to_all(results, 'dp', split_axis=0, concat_axis=3, tiled=True)  74.2 us
    all_gather x1, waiting for transfers between devices, local(): everyone = lax.all_gather(arrived, 'dp', axis=0, tiled=True)  70.2 us
    ppermute x7, waiting for transfers between devices, exchange_directly(): lax.ppermute(sent, axis, [(i, (i + lap) % peers) for i in range(peers)])  38.7 us
    all_to_all x2, local copies, waits for them, and re-layouts, local(): lax.all_to_all(results, 'dp', split_axis=0, concat_axis=3, tiled=True)  21.9 us
    ppermute x7, starting transfers between devices, exchange_directly(): lax.ppermute(sent, axis, [(i, (i + lap) % peers) for i in range(peers)])  16.8 us
    dot_general x1, matrix products, local(): jnp.einsum('sxcf,xfd->sxcd', everyone, down_weight, preferred_element_typ...  14.3 us
    gather x1, local copies, waits for them, and re-layouts, local(): pair_results = returned.reshape(experts * capacity, model_width)[slot_index]  12.3 us
  transfers between devices with their start and end apart: 9, of which 5 were waited for; matrix products, arithmetic and copies ran while one was open for 3% of the time, Pallas kernels for 0%

profile of v1, /device:TPU:0, one launch (start us, length us, event | category | flops | bytes accessed | tf_op | source)
XLA Modules:
  0.0 467.6 jit_solution(17987717781669559724)
XLA Ops:
  10.9 4.7 scatter_custom_fusion
  15.5 2.5 dynamic-slice_bitcast_fusion
  18.0 3.0 collective-permute-start
  21.0 3.0 collective-permute-start.6
  24.1 2.0 collective-permute-start.5
  26.1 3.0 collective-permute-start.3
  29.1 4.6 collective-permute-done
  33.6 1.6 collective-permute-start.1
  35.9 22.0 %collective-permute-done.1 = bf16[1,2,48,1536]{3,2,1,0:T(8,128)(2,1)S(1)} collective-permute-done((bf16[1,2,48,1536]{3,2,1,0:T(8,128)(2,1)S(1)}, bf16[1,2,48,1536]{3,2,1,0:T(8,128)(2,1)S(1)}, u32[]{:S(2)}, u32[]{:S(2)}) %collective-permute-start.1) | collective-permute-done | bytes 294944 | tf_op jit(solution)/shard_map/ppermute | solution.py:25
  57.9 4.2 collective-permute-start.2
  62.9 6.7 %collective-permute-done.2 = bf16[1,2,48,1536]{3,2,1,0:T(8,128)(2,1)S(1)} collective-permute-done((bf16[1,2,48,1536]{3,2,1,0:T(8,128)(2,1)S(1)}, bf16[1,2,48,1536]{3,2,1,0:T(8,128)(2,1)S(1)}, u32[]{:S(2)}, u32[]{:S(2)}) %collective-permute-start.2) | collective-permute-done | bytes 294944 | tf_op jit(solution)/shard_map/ppermute | solution.py:25
  70.3 5.4 %collective-permute-done.3 = bf16[1,2,48,1536]{3,2,1,0:T(8,128)(2,1)S(1)} collective-permute-done((bf16[1,2,48,1536]{3,2,1,0:T(8,128)(2,1)S(1)}, bf16[1,2,48,1536]{3,2,1,0:T(8,128)(2,1)S(1)}, u32[]{:S(2)}, u32[]{:S(2)}) %collective-permute-start.3) | collective-permute-done | bytes 294944 | tf_op jit(solution)/shard_map/ppermute | solution.py:25
  78.7 3.8 gather_fusion
  82.5 3.2 copy.18
  85.8 70.2 %all-gather.3.cloned.1.call-done = bf16[32,2,48,1536]{3,2,0,1:T(8,128)(2,1)} async-done(((bf16[8,2,48,1536]{3,2,0,1:T(8,128)(2,1)}), bf16[32,2,48,1536]{3,2,0,1:T(8,128)(2,1)}) %all-gather.3.cloned.1.call-update) | async-done | bytes 9437200 | tf_op jit(solution)/shard_map/all_gather | solution.py:55
  156.0 14.3 %convert_bitcast_fusion = bf16[32,2,48,1024]{3,2,0,1:T(8,128)(2,1)S(1)} fusion(bf16[32,2,48,1536]{3,2,0,1:T(8,128)(2,1)} %all-gather.3.cloned.1.call-done, bf16[2,1536,1024]{2,1,0:T(8,128)(2,1)} %param.7), kind=kOutput, calls=%fused_computation.8 | convolution fusion | flops 9666822144 | bytes 22020096 | tf_op jit(solution)/shard_map/sxcf,xfd->sxcd/dot_general | solution.py:66
  171.7 74.2 %all_to_all.23 = bf16[32,2,48,1024]{3,2,1,0:T(8,128)(2,1)} all-to-all(bf16[32,2,48,1024]{3,2,1,0:T(8,128)(2,1)S(1)} %copy.19), channel_id=1, replica_groups=mesh['dp'=4,'expert'=8] {'dp'}, dimensions={0} | all-to-all | bytes 12582912 | tf_op jit(solution)/shard_map/all_to_all | solution.py:70
  245.9 10.8 %copy.27 = bf16[4,8,2,48,1024]{4,0,3,2,1:T(4,128)(2,1)} copy(bf16[4,8,2,48,1024]{4,3,2,1,0:T(8,128)(2,1)} %bitcast.71) | data formatting | bytes 12582912 | tf_op jit(solution)/shard_map/all_to_all | solution.py:70
  256.7 11.1 %all_to_all.19 = bf16[8,2,48,4096]{3,2,1,0:T(8,128)(2,1)} reshape(bf16[8,2,48,4,1024]{4,3,2,1,0:T(4,128)(2,1)} %bitcast.72) | data formatting | bytes 12582912 | tf_op jit(solution)/shard_map/all_to_all | solution.py:70
  267.7 5.6 %all-to-all-start.1 = ((bf16[8,2,48,4096]{3,2,1,0:T(8,128)(2,1)}), bf16[8,2,48,4096]{3,2,1,0:T(8,128)(2,1)}, u32[]{:S(2)}, u32[]{:S(2)}) async-start(bf16[8,2,48,4096]{3,2,1,0:T(8,128)(2,1)} %all_to_all.19), calls=%async_computation.1 | async-start | bytes 12582912 | tf_op jit(solution)/shard_map/all_to_all | solution.py:69
  273.4 157.9 %psum.7 = f32[16]{0:T(128)S(1)} all-reduce(f32[16]{0:T(128)S(1)} %convert_element_type.36), channel_id=1, replica_groups=mesh['dp'=4,'expert'=8] {'dp','expert'}, use_global_device_ids=true, to_apply=%region_7.8 | all-reduce | flops 16 | bytes 128 | tf_op jit(solution)/shard_map/psum | solution.py:48
  431.5 10.5 %bitcast_divide_fusion = f32[2,384,1536]{2,1,0:T(8,128)} fusion(bf16[32,2,48,1536]{3,2,0,1:T(8,128)(2,1)} %all-gather.3.cloned.1.call-done, f32[2]{0:T(128)S(1)} %dynamic_slice.39, s32[]{:T(128)S(6)} %select_n.113), kind=kOutput, calls=%fused_computation.9 | convolution fusion | flops 3625058304 | bytes 16515084 | tf_op jit(solution)/shard_map/sxcf,sxcg->xfg/dot_general | solution.py:63
  442.0 12.3 %gather_fusion.1 = bf16[512,4096]{1,0:T(8,128)(2,1)} fusion(bf16[768,4096]{1,0:T(8,128)(2,1)} %bitcast.26, s32[1024]{0:T(1024)S(1)} %pad_clamp_fusion), kind=kCustom, calls=%fused_computation.1 | custom fusion | bytes 8390656 | tf_op jit(solution)/shard_map/gather | solution.py:78
  454.3 6.5 %fusion = bf16[64,4096]{1,0:T(8,128)(2,1)} fusion(bf16[512,4096]{1,0:T(8,128)(2,1)} %gather_fusion.1, f32[64,8]{1,0:T(8,128)S(1)} %copy.21), kind=kLoop, calls=%fused_computation.4 | loop fusion | flops 6029312 | bytes 4720640 | tf_op jit(solution)/shard_map/reduce_sum | solution.py:81
  (42 shorter events, 10.2 us)
Async XLA Ops:
  7.2 3.7 copy-start
  7.2 148.8 %all-gather.3.cloned.1.call-start = ((), (), s32[]{:S(2)}) async-start(), calls=%async_computation.2 | async-start | bytes 11796480 | tf_op jit(solution)/shard_map/all_gather | solution.py:55
  18.0 15.6 %collective-permute-start = (bf16[1,2,48,1536]{3,2,1,0:T(8,128)(2,1)S(1)}, bf16[1,2,48,1536]{3,2,1,0:T(8,128)(2,1)S(1)}, u32[]{:S(2)}, u32[]{:S(2)}) collective-permute-start(bf16[1,2,48,1536]{3,2,1,0:T(8,128)(2,1)S(1)} %get-tuple-element.10), channel_id=1, source_target_pairs={{0,1},{1,2},{2,3},{3,4},{4,5},{5,6},{6,7},{7,0},{8,9},{9,10},{10,1... | collective-permute-start | bytes 884744 | tf_op jit(solution)/shard_map/ppermute | solution.py:25
  21.0 56.9 %collective-permute-start.6 = (bf16[1,2,48,1536]{3,2,1,0:T(8,128)(2,1)S(1)}, bf16[1,2,48,1536]{3,2,1,0:T(8,128)(2,1)S(1)}, u32[]{:S(2)}, u32[]{:S(2)}) collective-permute-start(bf16[1,2,48,1536]{3,2,1,0:T(8,128)(2,1)S(1)} %get-tuple-element.4), channel_id=1, source_target_pairs={{0,7},{1,0},{2,1},{3,2},{4,3},{5,4},{6,5},{7,6},{8,15},{9,8},{10,9... | collective-permute-start | bytes 884744 | tf_op jit(solution)/shard_map/ppermute | solution.py:25
  24.1 53.2 %collective-permute-start.5 = (bf16[1,2,48,1536]{3,2,1,0:T(8,128)(2,1)S(1)}, bf16[1,2,48,1536]{3,2,1,0:T(8,128)(2,1)S(1)}, u32[]{:S(2)}, u32[]{:S(2)}) collective-permute-start(bf16[1,2,48,1536]{3,2,1,0:T(8,128)(2,1)S(1)} %get-tuple-element.5), channel_id=1, source_target_pairs={{0,6},{1,7},{2,0},{3,1},{4,2},{5,3},{6,4},{7,5},{8,14},{9,15},{10,... | collective-permute-start | bytes 884744 | tf_op jit(solution)/shard_map/ppermute | solution.py:25
  26.1 50.5 %collective-permute-start.4 = (bf16[1,2,48,1536]{3,2,1,0:T(8,128)(2,1)S(1)}, bf16[1,2,48,1536]{3,2,1,0:T(8,128)(2,1)S(1)}, u32[]{:S(2)}, u32[]{:S(2)}) collective-permute-start(bf16[1,2,48,1536]{3,2,1,0:T(8,128)(2,1)S(1)} %get-tuple-element.6), channel_id=1, source_target_pairs={{0,5},{1,6},{2,7},{3,0},{4,1},{5,2},{6,3},{7,4},{8,13},{9,14},{10,... | collective-permute-start | bytes 884744 | tf_op jit(solution)/shard_map/ppermute | solution.py:25
  26.1 49.7 %collective-permute-start.3 = (bf16[1,2,48,1536]{3,2,1,0:T(8,128)(2,1)S(1)}, bf16[1,2,48,1536]{3,2,1,0:T(8,128)(2,1)S(1)}, u32[]{:S(2)}, u32[]{:S(2)}) collective-permute-start(bf16[1,2,48,1536]{3,2,1,0:T(8,128)(2,1)S(1)} %get-tuple-element.7), channel_id=1, source_target_pairs={{0,4},{1,5},{2,6},{3,7},{4,0},{5,1},{6,2},{7,3},{8,12},{9,13},{10,... | collective-permute-start | bytes 884744 | tf_op jit(solution)/shard_map/ppermute | solution.py:25
  33.6 24.3 %collective-permute-start.1 = (bf16[1,2,48,1536]{3,2,1,0:T(8,128)(2,1)S(1)}, bf16[1,2,48,1536]{3,2,1,0:T(8,128)(2,1)S(1)}, u32[]{:S(2)}, u32[]{:S(2)}) collective-permute-start(bf16[1,2,48,1536]{3,2,1,0:T(8,128)(2,1)S(1)} %get-tuple-element.9), channel_id=1, source_target_pairs={{0,2},{1,3},{2,4},{3,5},{4,6},{5,7},{6,0},{7,1},{8,10},{9,11},{10,... | collective-permute-start | bytes 884744 | tf_op jit(solution)/shard_map/ppermute | solution.py:25
  57.9 11.7 %collective-permute-start.2 = (bf16[1,2,48,1536]{3,2,1,0:T(8,128)(2,1)S(1)}, bf16[1,2,48,1536]{3,2,1,0:T(8,128)(2,1)S(1)}, u32[]{:S(2)}, u32[]{:S(2)}) collective-permute-start(bf16[1,2,48,1536]{3,2,1,0:T(8,128)(2,1)S(1)} %get-tuple-element.8), channel_id=1, source_target_pairs={{0,3},{1,4},{2,5},{3,6},{4,7},{5,0},{6,1},{7,2},{8,11},{9,12},{10,... | collective-permute-start | bytes 884744 | tf_op jit(solution)/shard_map/ppermute | solution.py:25
  267.7 163.6 %copy-start.2 = (s32[64,8]{0,1:T(8,128)S(1)}, s32[64,8]{0,1:T(8,128)}, u32[]{:S(2)}) copy-start(s32[64,8]{0,1:T(8,128)} %param.6) | copy-start | bytes 6148
  267.7 174.3 %all-to-all-start.1 = ((bf16[8,2,48,4096]{3,2,1,0:T(8,128)(2,1)}), bf16[8,2,48,4096]{3,2,1,0:T(8,128)(2,1)}, u32[]{:S(2)}, u32[]{:S(2)}) async-start(bf16[8,2,48,4096]{3,2,1,0:T(8,128)(2,1)} %all_to_all.19), calls=%async_computation.1 | async-start | bytes 12582912 | tf_op jit(solution)/shard_map/all_to_all | solution.py:69
  442.0 18.7 %copy-start.1 = (bf16[64,8,1536]{2,1,0:T(8,128)(2,1)S(1)}, bf16[64,8,1536]{2,1,0:T(8,128)(2,1)}, u32[]{:S(2)}) copy-start(bf16[64,8,1536]{2,1,0:T(8,128)(2,1)} %param.4) | copy-start | bytes 4718596
Sparse Core Ops, SparseCore 0:
  85.9 70.0 all-gather.2
